TPU v7x, 32 devices: a whole 2x2x4 slice. The times are simulated.
32 devices in a mesh: blk: 8 (over y, x, core), cross: 4 (over z).
Axes of the slice: x: 2, y: 2, z: 4, core: 2. Of those that a mesh axis runs over, the one named last changes fastest.
Arguments:
- receiver_spectra: float32 [4096, 2, 1024], P(('blk', 'cross')), may hold values from -400 to 400
- source_spectra: float32 [4096, 2, 1024], P(('blk', 'cross')), may hold values from -400 to 400
- quality: int32 [4096], P(('blk', 'cross')), may hold values 0 or 1
- slot_order: int32 [32, 128], P(('blk', 'cross')), may hold values from 0 to 127, each once within a row
- owners: int32 [2, 8], replicated, may hold values from 0 to 3
Outputs:
- correlations: bfloat16 [2, 8, 4, 128, 128, 256], P(None, 'blk', 'cross')
Inputs may be any that keep to these rules, and one draw needn't show every extreme that they name: `slot_order`: each row is a permutation of 0 to 127.
All inputs are finite; a program needn't handle non-finite values. No bound on the sum of `quality` on one device may be relied on, other than what follows from the above.
Results may differ from a plain program's by a relative error of at most 0.0056.
Values sent between devices are 32-bit elements; how exact they have to be, the bound alone decides.
A program may use at most 128 MiB of HBM per device.

v0:
```python
import math
import jax
import jax.numpy as jnp
from jax import lax
from jax.sharding import PartitionSpec as P

L = 256
STEPS = 2


def passed_along(value, axis, steps):
    count = lax.axis_size(axis)
    pairs = [(source, (source + steps) % count) for source in range(count)]
    return lax.ppermute(value, axis, pairs)


def lag_tables(bins, lags):
    bin_index = jnp.arange(bins, dtype=jnp.int32)
    odd_index = 2 * jnp.arange(lags // 2, dtype=jnp.int32) + 1
    phase_turns = jnp.mod(bin_index[:, None] * odd_index[None, :], 4 * bins).astype(jnp.float32)
    phase_angle = phase_turns * (math.pi / (2 * bins))
    cos_table = (jnp.cos(phase_angle) / bins).astype(jnp.bfloat16)
    sin_table = (-jnp.sin(phase_angle) / bins).astype(jnp.bfloat16)
    return (cos_table, sin_table)


def whiten(spectra):
    mean_power = jnp.mean(spectra * spectra, axis=(1, 2), keepdims=True)
    return spectra * lax.rsqrt(mean_power + 1e-06)


def correlate(panel_spec, slab_spec, cos_table, sin_table):
    npanel = panel_spec.shape[0]
    nslab = slab_spec.shape[0]
    width = math.gcd(npanel, 16)
    blocks = panel_spec.reshape(npanel // width, width, 2, panel_spec.shape[2])

    def one_block(source):
        inphase = (
            source[:, None, 0, :] * slab_spec[None, :, 0, :]
            + source[:, None, 1, :] * slab_spec[None, :, 1, :]
        )
        quadrature = (
            source[:, None, 1, :] * slab_spec[None, :, 0, :]
            - source[:, None, 0, :] * slab_spec[None, :, 1, :]
        )
        inphase = inphase.astype(jnp.bfloat16).reshape(width * nslab, -1)
        quadrature = quadrature.astype(jnp.bfloat16).reshape(width * nslab, -1)
        even = jnp.dot(inphase, cos_table, preferred_element_type=jnp.float32)
        odd = jnp.dot(quadrature, sin_table, preferred_element_type=jnp.float32)
        joined = jnp.concatenate([even + odd, even - odd], axis=-1).astype(jnp.bfloat16)
        return joined.reshape(width, nslab, -1)

    lagged = lax.map(one_block, blocks)
    return lagged.reshape(npanel, nslab, lagged.shape[-1])


def local(receiver_spectra, source_spectra, quality, slot_order, owners):
    bins = receiver_spectra.shape[2]
    npanel = source_spectra.shape[0]
    cos_table, sin_table = lag_tables(bins, L)
    kept = quality.astype(jnp.float32)[:, None, None]
    receivers = whiten(receiver_spectra) * kept
    receivers = jnp.take(receivers, slot_order[0], axis=0)
    sources = whiten(source_spectra)
    block_index = lax.axis_index("blk")
    my_owners = lax.dynamic_index_in_dim(owners, block_index, 1, keepdims=False)
    every_panel = lax.all_gather(sources, "cross", axis=0, tiled=True)
    moving = receivers
    results = []
    for loop_step in range(STEPS):
        if loop_step > 0:
            moving = passed_along(moving, "blk", 1)
        owner_index = my_owners[loop_step]
        panel_spec = lax.dynamic_slice_in_dim(every_panel, owner_index * npanel, npanel, 0)
        results.append(correlate(panel_spec, moving, cos_table, sin_table))
    return jnp.stack(results)[:, None, None]


def solution(mesh):
    placed = (
        P(("blk", "cross"), None, None),
        P(("blk", "cross"), None, None),
        P(("blk", "cross")),
        P(("blk", "cross"), None),
        P(),
    )
    return jax.shard_map(
        local,
        mesh=mesh,
        in_specs=placed,
        out_specs=P(None, "blk", "cross", None, None, None),
        check_vma=False,
    )
```

profile of v0, /device:TPU:0, one launch (start us, length us, event | category | flops | bytes accessed | tf_op | source)
XLA Modules:
  0.0 305.8 jit_solution(16467009084390342149)
XLA Ops:
  6.5 2.3 multiply_reduce_fusion.1
  8.8 2.6 broadcast_multiply_fusion
  12.8 2.3 multiply_reduce_fusion
  15.1 1.7 multiply_multiply_fusion
  16.8 1.7 gather_fusion
  21.7 73.5 %all-gather.2.cloned.1.call-done = f32[512,2,1024]{2,1,0:T(2,128)} async-done(((f32[128,2,1024]{2,1,0:T(2,128)}), f32[512,2,1024]{2,1,0:T(2,128)}) %all-gather.2.cloned.1.call-update) | async-done | bytes 4194320 | tf_op jit(solution)/shard_map/all_gather | solution.py:68
  95.1 3.2 %constant_dynamic-slice_fusion.1 = (f32[128,2,1024]{2,1,0:T(2,128)S(1)}, f32[128,2,1024]{2,1,0:T(2,128)}) fusion(f32[512,2,1024]{2,1,0:T(2,128)} %all-gather.2.cloned.1.call-done, s32[]{:T(128)S(6)} %select_n.44, s32[]{:T(128)S(6)} %select_n.49), kind=kLoop, calls=%fused_computation.86 | loop fusion | bytes 4194312 | tf_op jit(solution)/shard_map/dynamic_slice | solution.py:75
  98.4 4.3 %broadcast.91.clone = bf16[8,16,128,256]{3,2,1,0:T(8,128)(2,1)} broadcast(bf16[]{:T(256)} %constant.66.clone.1), dimensions={} | broadcast | bytes 8388610 | tf_op jit(solution)/shard_map/broadcast.6
  102.6 92.7 %while.25 = (s32[]{:T(128)}, bf16[8,16,128,256]{3,2,1,0:T(8,128)(2,1)}, f32[8,16,2,1024]{3,2,1,0:T(2,128)}, f32[128,2,1024]{2,1,0:T(2,128)S(1)}, s32[128]{0:T(128)S(1)}, /*index=5*/s32[]{:T(128)}) while((s32[]{:T(128)}, bf16[8,16,128,256]{3,2,1,0:T(8,128)(2,1)}, f32[8,16,2,1024]{3,2,1,0:T(2,128)}, ...), condition=%wide.region_5.6_spmd.clone.clone, body=%wide.region_4.5_spmd.clone.clone.sunk | while | flops 1097990144 | bytes 28181588 | solution.py:54
  104.7 2.7 subtract_convert_fusion.7
  107.4 2.9 fusion.81
  110.3 2.8 add_convert_fusion.7
  116.3 2.7 subtract_convert_fusion.7
  119.0 2.9 fusion.81
  121.9 2.8 add_convert_fusion.7
  127.9 2.7 subtract_convert_fusion.7
  130.6 2.9 fusion.81
  133.4 2.8 add_convert_fusion.7
  139.5 2.7 subtract_convert_fusion.7
  142.1 2.9 fusion.81
  145.0 2.8 add_convert_fusion.7
  151.1 2.7 subtract_convert_fusion.7
  153.7 2.9 fusion.81
  156.6 2.8 add_convert_fusion.7
  162.6 2.7 subtract_convert_fusion.7
  165.3 2.9 fusion.81
  168.2 2.8 add_convert_fusion.7
  171.0 1.2 maximum_dynamic-update-slice_fusion.5
  174.2 2.7 subtract_convert_fusion.7
  176.9 2.9 fusion.81
  179.8 2.8 add_convert_fusion.7
  185.8 2.7 subtract_convert_fusion.7
  188.5 2.9 fusion.81
  191.4 2.8 add_convert_fusion.7
  194.2 1.2 maximum_dynamic-update-slice_fusion.5
  195.4 4.3 %broadcast.91.clone.1 = bf16[8,16,128,256]{3,2,1,0:T(8,128)(2,1)} broadcast(bf16[]{:T(256)} %constant.66.clone.1), dimensions={} | broadcast | bytes 8388610 | tf_op jit(solution)/shard_map/broadcast.6
  199.7 85.5 %while.24 = (s32[]{:T(128)}, bf16[8,16,128,256]{3,2,1,0:T(8,128)(2,1)}, f32[8,16,2,1024]{3,2,1,0:T(2,128)S(1)}, f32[128,2,1024]{2,1,0:T(2,128)S(1)}, s32[128]{0:T(128)S(1)}, /*index=5*/s32[]{:T(128)}) while((s32[]{:T(128)}, bf16[8,16,128,256]{3,2,1,0:T(8,128)(2,1)}, f32[8,16,2,1024]{3,2,1,0:T(2,128)S(1)}, ...), condition=%wide.region_3.4_spmd.clone.clone, body=%wide.region_2.3_spmd.clone.clone.sunk | while | flops 1097990144 | bytes 28181588 | solution.py:54
  200.8 2.7 subtract_convert_fusion.6
  203.5 2.9 fusion.76
  206.4 2.8 add_convert_fusion.6
  209.2 1.2 maximum_dynamic-update-slice_fusion.4
  211.6 2.7 subtract_convert_fusion.6
  214.3 2.9 fusion.76
  217.1 2.8 add_convert_fusion.6
  222.3 2.7 subtract_convert_fusion.6
  224.9 2.9 fusion.76
  227.8 2.8 add_convert_fusion.6
  232.9 2.7 subtract_convert_fusion.6
  235.6 2.9 fusion.76
  238.5 2.8 add_convert_fusion.6
  243.6 2.7 subtract_convert_fusion.6
  246.3 2.9 fusion.76
  249.2 2.8 add_convert_fusion.6
  252.0 1.2 maximum_dynamic-update-slice_fusion.4
  254.4 2.7 subtract_convert_fusion.6
  257.0 2.9 fusion.76
  259.9 2.8 add_convert_fusion.6
  265.0 2.7 subtract_convert_fusion.6
  267.7 2.9 fusion.76
  270.5 2.8 add_convert_fusion.6
  275.7 2.7 subtract_convert_fusion.6
  278.4 2.9 fusion.76
  281.2 2.8 add_convert_fusion.6
  285.2 13.8 %maximum_bitcast_fusion = bf16[2,1,1,128,128,256]{5,4,3,2,1,0:T(8,128)(2,1)} fusion(bf16[1,128,128,256]{3,2,1,0:T(8,128)(2,1)} %bitcast.87, bf16[1,128,128,256]{3,2,1,0:T(8,128)(2,1)} %bitcast.86), kind=kLoop, calls=%fused_computation.75 | loop fusion | flops 8388608 | bytes 33554432 | tf_op jit(solution)/shard_map/broadcast_in_dim | solution.py:77
  (112 shorter events, 42.5 us)
Async XLA Ops:
  6.5 13.2 %copy-start = (s32[2,8]{1,0:T(2,128)S(1)}, s32[2,8]{1,0:T(2,128)}, u32[]{:S(2)}) copy-start(s32[2,8]{1,0:T(2,128)} %param.13) | copy-start | bytes 196
  6.5 11.9 %copy-start.2 = (s32[1,128]{1,0:T(1,128)S(1)}, s32[1,128]{1,0:T(1,128)}, u32[]{:S(2)}) copy-start(s32[1,128]{1,0:T(1,128)} %param.12) | copy-start | bytes 1540
  6.5 88.6 %all-gather.2.cloned.1.call-start = ((), (), s32[]{:S(2)}) async-start(), calls=%async_computation | async-start | bytes 5242880 | tf_op jit(solution)/shard_map/all_gather | solution.py:68
  19.0 79.3 %collective-permute-start = (f32[128,2,1024]{2,1,0:T(2,128)S(1)}, f32[128,2,1024]{2,1,0:T(2,128)S(1)}, u32[]{:S(2)}, u32[]{:S(2)}) collective-permute-start(f32[128,2,1024]{2,1,0:T(2,128)S(1)} %broadcast_select_fusion), channel_id=1, source_target_pairs={{0,4},{4,8},{8,12},{12,16},{16,20},{20,24},{24,28},{28,0},{1,5},{5... | collective-permute-start | bytes 3145736 | tf_op jit(solution)/shard_map/ppermute | solution.py:14
  285.2 13.8 %copy-start.1 = (s32[2,8]{1,0:T(2,128)S(1)}, s32[2,8]{1,0:T(2,128)}, u32[]{:S(2)}) copy-start(s32[2,8]{1,0:T(2,128)} %param.13) | copy-start | bytes 196
Sparse Core Ops, SparseCore 0:
  11.6 83.4 all-gather.1
where the time goes:
time: 306 us
  matrix products  90.8 us (30%)
  other arithmetic  85.6 us (28%)
  waiting for transfers between devices  73.5 us (24%)
  local copies, waits for them, and re-layouts  39.7 us (13%)
  between operations  14.7 us (5%)
    all_gather x1, waiting for transfers between devices, local(): every_panel = lax.all_gather(sources, 'cross', axis=0, tiled=True)  73.5 us
    dot_general x16, matrix products, one_block(): odd = jnp.dot(quadrature, sin_table, preferred_element_type=jnp.float32)  45.8 us
    dot_general x16, matrix products, one_block(): even = jnp.dot(inphase, cos_table, preferred_element_type=jnp.float32)  45 us
    convert_element_type x16, other arithmetic, one_block(): quadrature = quadrature.astype(jnp.bfloat16).reshape(width * nslab, -1)  42.7 us
    dynamic_update_slice x16, other arithmetic, correlate(): lagged = lax.map(one_block, blocks)  18.4 us
    broadcast_in_dim x1, other arithmetic, local(): return jnp.stack(results)[:, None, None]  13.8 us
    slice x16, local copies, waits for them, and re-layouts, one_block(): slab_spec[None, :, 0, :]  13 us
    another operation x2, local copies, waits for them, and re-layouts  8.57 us
  transfers between devices with their start and end apart: 2, of which 1 were waited for; matrix products, arithmetic and copies ran while one was open for 4% of the time, Pallas kernels for 0%

commit v1 on v0

--- a/solution.py
+++ b/solution.py
@@ -6,6 +6,28 @@
 
 L = 256
 STEPS = 2
+
+
+def in_order(parts, dim):
+    lengths = list(parts.shape[1:])
+    lengths[dim] *= parts.shape[0]
+    return jnp.moveaxis(parts, 0, dim).reshape(lengths)
+
+
+def collect(x, axis, dim):
+    peers = lax.axis_size(axis)
+    pairs = [(i, (i + 1) % peers) for i in range(peers)]
+    back = [(b, a) for a, b in pairs]
+    lower, upper = ([], [])
+    for step in range(peers - 1):
+        if step % 2 == 0:
+            lower.append(lax.ppermute(lower[-1] if lower else x, axis, pairs))
+        else:
+            upper.append(lax.ppermute(upper[-1] if upper else x, axis, back))
+    blocks = jnp.stack([*lower[::-1], x, *upper])
+    shift = lax.axis_index(axis) - len(lower)
+    blocks = blocks[(jnp.arange(peers) - shift) % peers]
+    return in_order(blocks, dim)
 
 
 def passed_along(value, axis, steps):
@@ -65,7 +87,7 @@
     sources = whiten(source_spectra)
     block_index = lax.axis_index("blk")
     my_owners = lax.dynamic_index_in_dim(owners, block_index, 1, keepdims=False)
-    every_panel = lax.all_gather(sources, "cross", axis=0, tiled=True)
+    every_panel = collect(sources, "cross", 0)
     moving = receivers
     results = []
     for loop_step in range(STEPS):

time: 306 us -> 300 us (0.980)
  between operations: 14.7 us -> 1.46 us
  waiting for transfers between devices: 73.5 us -> 60.5 us
  local copies, waits for them, and re-layouts: 39.7 us -> 48.1 us
  starting transfers between devices: 0.73 us -> 6.76 us
  other arithmetic: 85.6 us -> 91.2 us
    all_gather x1 -> x0, waiting for transfers between devices: 73.5 us -> none  [local(): every_panel = lax.all_gather(sources, 'cross', axis=0, tiled=True)]
    ppermute x0 -> x3, waiting for transfers between devices: none -> 60.5 us  [the longest x2 60.5 us: collect(): lower.append(lax.ppermute(lower[-1] if lower else x, axis, pairs))]
    gather x0 -> x1, local copies, waits for them, and re-layouts: none -> 8.36 us  [collect(): blocks = blocks[(jnp.arange(peers) - shift) % peers]]
    ppermute x0 -> x3, starting transfers between devices: none -> 6.7 us  [the longest x1 5.08 us: collect(): upper.append(lax.ppermute(upper[-1] if upper else x, axis, back))]
    another operation x0 -> x2, other arithmetic: none -> 5.63 us  [collect(): blocks = jnp.stack([*lower[::-1], x, *upper])]
  transfers between devices with their start and end apart: 2 -> 4, of which waited for: 1 -> 2; matrix products, arithmetic and copies ran while one was open for 4% -> 8% of each run, Pallas kernels for 0% -> 0%
where the time goes in v1:
time: 300 us
  other arithmetic  91.2 us (30%)
  matrix products  90.8 us (30%)
  waiting for transfers between devices  60.5 us (20%)
  local copies, waits for them, and re-layouts  48.1 us (16%)
  starting transfers between devices  6.76 us (2%)
    ppermute x2, waiting for transfers between devices, collect(): lower.append(lax.ppermute(lower[-1] if lower else x, axis, pairs))  60.5 us
    dot_general x16, matrix products, one_block(): odd = jnp.dot(quadrature, sin_table, preferred_element_type=jnp.float32)  45.8 us
    dot_general x16, matrix products, one_block(): even = jnp.dot(inphase, cos_table, preferred_element_type=jnp.float32)  45 us
    convert_element_type x16, other arithmetic, one_block(): quadrature = quadrature.astype(jnp.bfloat16).reshape(width * nslab, -1)  42.6 us
    dynamic_update_slice x16, other arithmetic, correlate(): lagged = lax.map(one_block, blocks)  18.4 us
    broadcast_in_dim x1, other arithmetic, local(): return jnp.stack(results)[:, None, None]  13.8 us
    slice x16, local copies, waits for them, and re-layouts, one_block(): slab_spec[None, :, 0, :]  13 us
    another operation x2, local copies, waits for them, and re-layouts  8.57 us
  transfers between devices with their start and end apart: 4, of which 2 were waited for; matrix products, arithmetic and copies ran while one was open for 8% of the time, Pallas kernels for 0%

profile of v1, /device:TPU:0, one launch (start us, length us, event | category | flops | bytes accessed | tf_op | source)
XLA Modules:
  0.0 299.8 jit_solution(6217098043048838610)
XLA Ops:
  0.0 2.4 multiply_reduce_fusion.1
  2.4 2.6 broadcast_multiply_fusion
  5.0 5.1 %collective-permute-start.2 = (f32[128,2,1024]{2,1,0:T(2,128)}, f32[128,2,1024]{2,1,0:T(2,128)}, u32[]{:S(2)}, u32[]{:S(2)}) collective-permute-start(f32[128,2,1024]{2,1,0:T(2,128)} %broadcast_multiply_fusion), channel_id=1, source_target_pairs={{1,0},{2,1},{3,2},{0,3},{5,4},{6,5},{7,6},{4,7},{9,8},{10,9},{11,1... | collective-permute-start | bytes 3145736 | tf_op jit(solution)/shard_map/ppermute | solution.py:26
  11.4 2.3 multiply_reduce_fusion
  13.7 1.7 multiply_multiply_fusion
  15.4 1.7 gather_fusion.1
  17.1 39.1 %collective-permute-done = f32[128,2,1024]{2,1,0:T(2,128)} collective-permute-done((f32[128,2,1024]{2,1,0:T(2,128)}, f32[128,2,1024]{2,1,0:T(2,128)}, u32[]{:S(2)}, u32[]{:S(2)}) %collective-permute-start) | collective-permute-done | bytes 1048608 | tf_op jit(solution)/shard_map/ppermute | solution.py:24
  60.9 21.4 %collective-permute-done.1 = f32[128,2,1024]{2,1,0:T(2,128)} collective-permute-done((f32[128,2,1024]{2,1,0:T(2,128)}, f32[128,2,1024]{2,1,0:T(2,128)}, u32[]{:S(2)}, u32[]{:S(2)}) %collective-permute-start.1) | collective-permute-done | bytes 1048608 | tf_op jit(solution)/shard_map/ppermute | solution.py:24
  82.4 5.2 %pad_maximum_fusion = f32[4,128,2,1024]{3,2,1,0:T(2,128)} fusion(f32[1,128,2,1024]{3,2,1,0:T(2,128)} %bitcast.3, f32[1,128,2,1024]{3,2,1,0:T(2,128)S(1)} %fusion.64, f32[1,128,2,1024]{3,2,1,0:T(2,128)} %bitcast.1, f32[1,128,2,1024]{3,2,1,0:T(2,128)} %bitcast), kind=kLoop, calls=%fused_computation.77 | loop fusion | flops 3145728 | bytes 8388608 | tf_op jit(solution)/shard_map/stack | solution.py:27
  87.6 8.4 %gather_fusion = f32[4,128,2,1024]{3,2,1,0:T(2,128)} fusion(f32[4,128,2,1024]{3,2,1,0:T(2,128)} %pad_maximum_fusion, s32[1024]{0:T(1024)S(1)} %pad_clamp_fusion.1), kind=kCustom, calls=%fused_computation | custom fusion | bytes 8388624 | tf_op jit(solution)/shard_map/gather | solution.py:29
  95.9 3.2 %constant_dynamic-slice_fusion.1 = (f32[128,2,1024]{2,1,0:T(2,128)S(1)}, f32[128,2,1024]{2,1,0:T(2,128)}) fusion(f32[512,2,1024]{2,1,0:T(2,128)} %bitcast.100, s32[]{:T(128)S(6)} %select_n.69, s32[]{:T(128)S(6)} %select_n.74), kind=kLoop, calls=%fused_computation.93 | loop fusion | bytes 4194312 | tf_op jit(solution)/shard_map/dynamic_slice | solution.py:97
  99.1 4.3 %broadcast.154.clone = bf16[8,16,128,256]{3,2,1,0:T(8,128)(2,1)} broadcast(bf16[]{:T(256)} %constant.84.clone.1), dimensions={} | broadcast | bytes 8388610 | tf_op jit(solution)/shard_map/broadcast.10
  103.4 92.7 %while.25 = (s32[]{:T(128)}, bf16[8,16,128,256]{3,2,1,0:T(8,128)(2,1)}, f32[8,16,2,1024]{3,2,1,0:T(2,128)}, f32[128,2,1024]{2,1,0:T(2,128)S(1)}, s32[128]{0:T(128)S(1)}, /*index=5*/s32[]{:T(128)}) while((s32[]{:T(128)}, bf16[8,16,128,256]{3,2,1,0:T(8,128)(2,1)}, f32[8,16,2,1024]{3,2,1,0:T(2,128)}, ...), condition=%wide.region_5.6_spmd.clone.clone, body=%wide.region_4.5_spmd.clone.clone.sunk | while | flops 1097990144 | bytes 28181588 | solution.py:76
  105.5 2.7 subtract_convert_fusion.7
  108.2 2.9 fusion.84
  111.1 2.8 add_convert_fusion.7
  117.1 2.7 subtract_convert_fusion.7
  119.8 2.9 fusion.84
  122.6 2.8 add_convert_fusion.7
  128.7 2.7 subtract_convert_fusion.7
  131.4 2.9 fusion.84
  134.2 2.8 add_convert_fusion.7
  140.3 2.7 subtract_convert_fusion.7
  142.9 2.9 fusion.84
  145.8 2.8 add_convert_fusion.7
  151.9 2.7 subtract_convert_fusion.7
  154.5 2.9 fusion.84
  157.4 2.8 add_convert_fusion.7
  163.4 2.7 subtract_convert_fusion.7
  166.1 2.9 fusion.84
  169.0 2.8 add_convert_fusion.7
  175.0 2.7 subtract_convert_fusion.7
  177.7 2.9 fusion.84
  180.6 2.8 add_convert_fusion.7
  186.6 2.7 subtract_convert_fusion.7
  189.3 2.9 fusion.84
  192.2 2.8 add_convert_fusion.7
  196.2 4.3 %broadcast.154.clone.1 = bf16[8,16,128,256]{3,2,1,0:T(8,128)(2,1)} broadcast(bf16[]{:T(256)} %constant.84.clone.1), dimensions={} | broadcast | bytes 8388610 | tf_op jit(solution)/shard_map/broadcast.10
  200.4 85.5 %while.24 = (s32[]{:T(128)}, bf16[8,16,128,256]{3,2,1,0:T(8,128)(2,1)}, f32[8,16,2,1024]{3,2,1,0:T(2,128)S(1)}, f32[128,2,1024]{2,1,0:T(2,128)S(1)}, s32[128]{0:T(128)S(1)}, /*index=5*/s32[]{:T(128)}) while((s32[]{:T(128)}, bf16[8,16,128,256]{3,2,1,0:T(8,128)(2,1)}, f32[8,16,2,1024]{3,2,1,0:T(2,128)S(1)}, ...), condition=%wide.region_3.4_spmd.clone.clone, body=%wide.region_2.3_spmd.clone.clone.sunk | while | flops 1097990144 | bytes 28181588 | solution.py:76
  201.6 2.7 subtract_convert_fusion.6
  204.3 2.9 fusion.79
  207.2 2.8 add_convert_fusion.6
  212.4 2.7 subtract_convert_fusion.6
  215.0 2.9 fusion.79
  217.9 2.8 add_convert_fusion.6
  223.0 2.7 subtract_convert_fusion.6
  225.7 2.9 fusion.79
  228.6 2.8 add_convert_fusion.6
  233.7 2.7 subtract_convert_fusion.6
  236.4 2.9 fusion.79
  239.2 2.8 add_convert_fusion.6
  244.4 2.7 subtract_convert_fusion.6
  247.1 2.9 fusion.79
  249.9 2.8 add_convert_fusion.6
  255.1 2.7 subtract_convert_fusion.6
  257.8 2.9 fusion.79
  260.6 2.8 add_convert_fusion.6
  265.8 2.7 subtract_convert_fusion.6
  268.4 2.9 fusion.79
  271.3 2.8 add_convert_fusion.6
  276.4 2.7 subtract_convert_fusion.6
  279.1 2.9 fusion.79
  282.0 2.8 add_convert_fusion.6
  285.9 13.8 %maximum_bitcast_fusion = bf16[2,1,1,128,128,256]{5,4,3,2,1,0:T(8,128)(2,1)} fusion(bf16[1,128,128,256]{3,2,1,0:T(8,128)(2,1)} %bitcast.95, bf16[1,128,128,256]{3,2,1,0:T(8,128)(2,1)} %bitcast.94), kind=kLoop, calls=%fused_computation.76 | loop fusion | flops 8388608 | bytes 33554432 | tf_op jit(solution)/shard_map/broadcast_in_dim | solution.py:99
  (122 shorter events, 48.7 us)
Async XLA Ops:
  0.0 58.4 %copy-start = (s32[2,8]{1,0:T(2,128)S(1)}, s32[2,8]{1,0:T(2,128)}, u32[]{:S(2)}) copy-start(s32[2,8]{1,0:T(2,128)} %param.13) | copy-start | bytes 196
  0.0 60.5 %copy-start.2 = (f32[128,2,1024]{2,1,0:T(2,128)S(1)}, f32[128,2,1024]{2,1,0:T(2,128)}, u32[]{:S(2)}) copy-start(f32[128,2,1024]{2,1,0:T(2,128)} %param.10) | copy-start | bytes 3145732
  0.0 17.1 %copy-start.3 = (s32[1,128]{1,0:T(1,128)S(1)}, s32[1,128]{1,0:T(1,128)}, u32[]{:S(2)}) copy-start(s32[1,128]{1,0:T(1,128)} %param.12) | copy-start | bytes 1540
  5.0 55.9 %collective-permute-start.2 = (f32[128,2,1024]{2,1,0:T(2,128)}, f32[128,2,1024]{2,1,0:T(2,128)}, u32[]{:S(2)}, u32[]{:S(2)}) collective-permute-start(f32[128,2,1024]{2,1,0:T(2,128)} %broadcast_multiply_fusion), channel_id=1, source_target_pairs={{1,0},{2,1},{3,2},{0,3},{5,4},{6,5},{7,6},{4,7},{9,8},{10,9},{11,1... | collective-permute-start | bytes 3145736 | tf_op jit(solution)/shard_map/ppermute | solution.py:26
  10.1 46.1 %collective-permute-start = (f32[128,2,1024]{2,1,0:T(2,128)}, f32[128,2,1024]{2,1,0:T(2,128)}, u32[]{:S(2)}, u32[]{:S(2)}) collective-permute-start(f32[128,2,1024]{2,1,0:T(2,128)} %broadcast_multiply_fusion), channel_id=1, source_target_pairs={{0,1},{1,2},{2,3},{3,0},{4,5},{5,6},{6,7},{7,4},{8,9},{9,10},{10,1... | collective-permute-start | bytes 3145736 | tf_op jit(solution)/shard_map/ppermute | solution.py:24
  56.2 26.2 %collective-permute-start.1 = (f32[128,2,1024]{2,1,0:T(2,128)}, f32[128,2,1024]{2,1,0:T(2,128)}, u32[]{:S(2)}, u32[]{:S(2)}) collective-permute-start(f32[128,2,1024]{2,1,0:T(2,128)} %collective-permute-done), channel_id=1, source_target_pairs={{0,1},{1,2},{2,3},{3,0},{4,5},{5,6},{6,7},{7,4},{8,9},{9,10},{10,1... | collective-permute-start | bytes 3145736 | tf_op jit(solution)/shard_map/ppermute | solution.py:24
  58.4 40.8 %collective-permute-start.3 = (f32[128,2,1024]{2,1,0:T(2,128)S(1)}, f32[128,2,1024]{2,1,0:T(2,128)S(1)}, u32[]{:S(2)}, u32[]{:S(2)}) collective-permute-start(f32[128,2,1024]{2,1,0:T(2,128)S(1)} %broadcast_select_fusion), channel_id=1, source_target_pairs={{0,4},{4,8},{8,12},{12,16},{16,20},{20,24},{24,28},{28,0},{1,5},{5... | collective-permute-start | bytes 3145736 | tf_op jit(solution)/shard_map/ppermute | solution.py:36
  285.9 13.8 %copy-start.1 = (s32[2,8]{1,0:T(2,128)S(1)}, s32[2,8]{1,0:T(2,128)}, u32[]{:S(2)}) copy-start(s32[2,8]{1,0:T(2,128)} %param.13) | copy-start | bytes 196
